TPU v7x, 32 devices: a whole 2x2x4 slice. The times are simulated.
32 devices in a mesh: cuts: 2 (over core), lx: 2 (over x), ly: 8 (over z, y).
Axes of the slice: x: 2, y: 2, z: 4, core: 2. Of those that a mesh axis runs over, the one named last changes fastest.
Arguments:
- disorder: int32 [16, 16, 128], P('lx', 'ly'), may hold values from 0 to 255
- slice_bounds: float32 [12, 2], P('cuts'), may hold values from -1.5 to 1.5
- start: float32 [12, 32, 16, 16, 128], P('cuts', None, 'lx', 'ly'), may hold values from -36 to 36
- ritz: float32 [12, 8, 16, 16, 128], P('cuts', None, 'lx', 'ly'), may hold values from -4 to 4
Outputs:
- block: float32 [12, 32, 16, 16, 128], P('cuts', None, 'lx', 'ly')
- correlations: float32 [12, 16, 32], P('cuts')
All inputs are finite; a program needn't handle non-finite values.
Results may differ from a plain program's by a relative error of at most 0.000096.
Values sent between devices are 32-bit elements; how exact they have to be, the bound alone decides.
A program may use at most 64 MiB of HBM per device.

v0:
```python
import jax
import jax.numpy as jnp
from jax import lax
from jax.sharding import PartitionSpec as P

LEVELS = 256


def passed_along(value, axis, steps):
    count = lax.axis_size(axis)
    first, last = (max(0, -steps), min(count, count - steps))
    return lax.ppermute(value, axis, [(source, source + steps) for source in range(first, last)])


def padded_2(block, sides, width):
    for axis, dim in sides:
        count = lax.axis_size(axis)
        forward = [(i, i + 1) for i in range(count - 1)]
        forward.append((count - 1, 0))
        backward = [(target, source) for source, target in forward]
        low = lax.ppermute(
            lax.slice_in_dim(block, block.shape[dim] - width, None, axis=dim), axis, forward
        )
        high = lax.ppermute(lax.slice_in_dim(block, 0, width, axis=dim), axis, backward)
        block = jnp.concatenate([low, block, high], axis=dim)
    return block


def apply_scaled(field, onsite, centre):
    inner = field[:, 1:-1, 1:-1]
    beside = field[:, 2:, 1:-1] + field[:, :-2, 1:-1]
    beside = beside + field[:, 1:-1, 2:] + field[:, 1:-1, :-2]
    beside = beside + jnp.roll(inner, 1, 3) + jnp.roll(inner, -1, 3)
    return ((onsite[None] - centre) * inner - beside) / 16.0


def on_device(disorder, slice_bounds, start, ritz):
    onsite = 16.5 * (disorder.astype(jnp.float32) / jnp.float32(LEVELS - 1) - 0.5)
    count = start.shape[0]
    width = start.shape[1]
    centre = jnp.repeat((slice_bounds[:, 0] + slice_bounds[:, 1]) / 2.0, width)[:, None, None, None]
    vectors = start.reshape((count * width,) + start.shape[2:])
    lower_edge = passed_along(ritz[-1:], "cuts", 1)
    upper_edge = passed_along(ritz[:1], "cuts", -1)
    lower = jnp.concatenate([lower_edge, ritz[:-1]], 0)
    upper = jnp.concatenate([ritz[1:], upper_edge], 0)

    def filter_step(field):
        padded = padded_2(field, (("lx", 1), ("ly", 2)), 1)
        return apply_scaled(padded, onsite, centre)

    previous = vectors
    current = filter_step(vectors)
    previous, current = (current, 2.0 * filter_step(current) - previous)
    shape = current.shape
    cells = shape[1] * shape[2] * shape[3]
    total = jnp.float32(cells * lax.axis_size("lx") * lax.axis_size("ly"))
    hp = lax.Precision.HIGHEST
    filtered = current.reshape(count, width, cells)
    window = jnp.concatenate([lower, upper], 1).reshape(count, 2 * ritz.shape[1], cells)
    summed = lax.psum(jnp.einsum("src,svc->srv", window, filtered, precision=hp), ("lx", "ly"))
    correlation = summed / total
    cleaned = filtered - jnp.einsum("srv,src->svc", correlation, window, precision=hp)
    gram = lax.psum(jnp.einsum("sac,sbc->sab", cleaned, cleaned, precision=hp), ("lx", "ly"))
    factor = jnp.linalg.cholesky(gram / total)
    result = jax.scipy.linalg.solve_triangular(factor, cleaned, lower=True)
    return (result.reshape((count, width) + shape[1:]), correlation)


def solution(mesh):
    in_specs = (
        P("lx", "ly", None),
        P("cuts", None),
        P("cuts", None, "lx", "ly", None),
        P("cuts", None, "lx", "ly", None),
    )
    out_specs = (P("cuts", None, "lx", "ly", None), P("cuts", None, None))
    return jax.shard_map(
        on_device, mesh=mesh, in_specs=in_specs, out_specs=out_specs, check_vma=False
    )
```

profile of v0, /device:TPU:0, one launch (start us, length us, event | category | flops | bytes accessed | tf_op | source)
XLA Modules:
  0.0 334.0 jit_solution(6009458818156026938)
XLA Ops:
  1.7 3.0 collective-permute-start
  10.5 3.4 %collective-permute-done.1 = f32[192,1,2,128]{3,2,1,0:T(2,128)S(1)} collective-permute-done((f32[192,1,2,128]{3,2,1,0:T(2,128)S(1)}, f32[192,1,2,128]{3,2,1,0:T(2,128)S(1)}, u32[]{:S(2)}, u32[]{:S(2)}) %collective-permute-start.1) | collective-permute-done | bytes 196640 | tf_op jit(solution)/shard_map/ppermute | solution.py:21
  18.1 4.9 %collective-permute-start.2 = (f32[192,10,1,128]{3,2,1,0:T(1,128)S(1)}, f32[192,10,1,128]{3,2,1,0:T(1,128)}, u32[]{:S(2)}, u32[]{:S(2)}) collective-permute-start(f32[192,10,1,128]{3,2,1,0:T(1,128)S(1)} %get-tuple-element.4), channel_id=1, source_target_pairs={{1,0},{2,1},{3,2},{4,3},{5,4},{6,5},{7,6},{0,7},{9,8},{10,9},{11,1... | collective-permute-start | bytes 2949128 | tf_op jit(solution)/shard_map/ppermute | solution.py:24
  23.8 2.1 fusion.23
  26.0 2.1 fusion.24
  28.2 34.1 %collective-permute-done.2 = f32[192,10,1,128]{3,2,1,0:T(1,128)} collective-permute-done((f32[192,10,1,128]{3,2,1,0:T(1,128)S(1)}, f32[192,10,1,128]{3,2,1,0:T(1,128)}, u32[]{:S(2)}, u32[]{:S(2)}) %collective-permute-start.2) | collective-permute-done | bytes 983072 | tf_op jit(solution)/shard_map/ppermute | solution.py:24
  62.3 9.1 %fusion.1 = f32[192,8,2,128]{3,2,1,0:T(2,128)S(1)} fusion(f32[192,8,2,128]{3,2,1,0:T(2,128)S(1)} %bitcast.24, f32[192,10,1,128]{3,2,1,0:T(1,128)} %collective-permute-done.3, f32[192,1,2,128]{3,2,1,0:T(2,128)S(1)} %copy-done.4, f32[192,1,2,128]{3,2,1,0:T(2,128)S(1)} %copy-done.6, f32[192,10,1,128]{3,2,1,0:T(1,128)} %collective-permute-done.2, ...), kind=kLoop, calls=%fused_computation.6 | loop fusion | flops 7471104 | bytes 8659712 | tf_op jit(solution)/shard_map/div | solution.py:34
  73.8 5.6 %collective-permute-done.4 = f32[192,1,2,128]{3,2,1,0:T(2,128)S(1)} collective-permute-done((f32[192,1,2,128]{3,2,1,0:T(2,128)S(1)}, f32[192,1,2,128]{3,2,1,0:T(2,128)S(1)}, u32[]{:S(2)}, u32[]{:S(2)}) %collective-permute-start.4) | collective-permute-done | bytes 196640 | tf_op jit(solution)/shard_map/ppermute | solution.py:24
  79.3 3.0 collective-permute-done.5
  83.3 2.8 fusion.18
  86.1 2.8 collective-permute-start.6
  88.9 2.1 maximum_maximum_fusion
  91.0 2.6 reshape.34
  93.6 2.1 fusion.20
  95.8 2.1 fusion.21
  98.0 33.2 %collective-permute-done.6 = f32[192,10,1,128]{3,2,1,0:T(1,128)} collective-permute-done((f32[192,10,1,128]{3,2,1,0:T(1,128)}, f32[192,10,1,128]{3,2,1,0:T(1,128)}, u32[]{:S(2)}, u32[]{:S(2)}) %collective-permute-start.6) | collective-permute-done | bytes 983072 | tf_op jit(solution)/shard_map/ppermute | solution.py:24
  131.1 10.1 %fusion.4 = f32[192,8,2,128]{3,2,1,0:T(2,128)} fusion(f32[192,8,2,128]{3,2,1,0:T(2,128)S(1)} %fusion.1, f32[192,10,1,128]{3,2,1,0:T(1,128)} %collective-permute-done.7, f32[192,1,2,128]{3,2,1,0:T(2,128)S(1)} %collective-permute-done.4, f32[192,1,2,128]{3,2,1,0:T(2,128)S(1)} %collective-permute-done.5, f32[192,10,1,128]{3,2,1,0:T(1,128)} %collective-permute-done.6, ...), kind=kLoop, calls=%fused_computation.9 | loop fusion | flops 7864320 | bytes 10232576 | tf_op jit(solution)/shard_map/sub | solution.py:54
  141.2 2.6 reshape.33
  145.2 75.1 %psum.14 = f32[6,16,32]{2,1,0:T(8,128)S(1)} all-reduce(f32[6,16,32]{2,1,0:T(8,128)S(1)} %fusion.28), channel_id=1, replica_groups=mesh['cuts'=2,'lx'=2,'ly'=8] {'lx','ly'}, use_global_device_ids=true, to_apply=%region_0.1 | all-reduce | flops 3072 | bytes 24576 | tf_op jit(solution)/shard_map/psum | solution.py:61
  220.4 2.6 convolution_subtract_fusion
  224.5 72.8 %psum.15 = f32[6,32,32]{1,2,0:T(8,128)S(1)} all-reduce(f32[6,32,32]{1,2,0:T(8,128)S(1)} %fusion.29), channel_id=1, replica_groups=mesh['cuts'=2,'lx'=2,'ly'=8] {'lx','ly'}, use_global_device_ids=true, to_apply=%region_1.2 | all-reduce | flops 6144 | bytes 49152 | tf_op jit(solution)/shard_map/psum | solution.py:64
  297.4 17.6 %custom-call.8 = f32[6,32,32]{2,1,0:T(8,128)S(1)} custom-call(f32[6,32,32]{2,1,0:T(8,128)S(1)} %fusion.17), custom_call_target="Cholesky" | custom-call | tf_op jit(solution)/shard_map/jit(cholesky)/cholesky | solution.py:65
  315.2 14.8 %custom-call.9 = f32[6,1,32,32]{2,3,1,0:T(8,128)S(1)} custom-call(f32[6,1,32,32]{3,2,1,0:T(8,128)S(1)} %select_bitcast_fusion), custom_call_target="InvertDiagBlocksLowerTriangular" | custom-call | tf_op jit(solution)/shard_map/jit(_solve_triangular)/vmap()/triangular_solve | solution.py:66
  331.5 2.5 reshape.35
  (57 shorter events, 20.0 us)
Async XLA Ops:
  1.7 8.8 %collective-permute-start = (f32[192,1,2,128]{3,2,1,0:T(2,128)S(1)}, f32[192,1,2,128]{3,2,1,0:T(2,128)S(1)}, u32[]{:S(2)}, u32[]{:S(2)}) collective-permute-start(f32[192,1,2,128]{3,2,1,0:T(2,128)S(1)} %get-tuple-element.17), channel_id=1, source_target_pairs={{8,0},{0,8},{9,1},{1,9},{10,2},{2,10},{11,3},{3,11},{12,4},{4,12},... | collective-permute-start | bytes 589832 | tf_op jit(solution)/shard_map/ppermute | solution.py:24
  4.7 9.1 %collective-permute-start.1 = (f32[192,1,2,128]{3,2,1,0:T(2,128)S(1)}, f32[192,1,2,128]{3,2,1,0:T(2,128)S(1)}, u32[]{:S(2)}, u32[]{:S(2)}) collective-permute-start(f32[192,1,2,128]{3,2,1,0:T(2,128)S(1)} %get-tuple-element.16), channel_id=1, source_target_pairs={{0,8},{8,0},{1,9},{9,1},{2,10},{10,2},{3,11},{11,3},{4,12},{12,4},... | collective-permute-start | bytes 589832 | tf_op jit(solution)/shard_map/ppermute | solution.py:21
  6.3 82.5 %collective-permute-start.8 = (f32[1,8,8,2,128]{4,3,2,1,0:T(2,128)}, f32[1,8,8,2,128]{4,3,2,1,0:T(2,128)}, u32[]{:S(2)}, u32[]{:S(2)}) collective-permute-start(f32[1,8,8,2,128]{4,3,2,1,0:T(2,128)} %get-tuple-element.18), channel_id=1, source_target_pairs={{0,16},{1,17},{2,18},{3,19},{4,20},{5,21},{6,22},{7,23},{8,24},{9,... | collective-permute-start | bytes 196616 | tf_op jit(solution)/shard_map/ppermute | solution.py:12
  8.4 80.5 %collective-permute-start.9 = (f32[1,8,8,2,128]{4,3,2,1,0:T(2,128)}, f32[1,8,8,2,128]{4,3,2,1,0:T(2,128)}, u32[]{:S(2)}, u32[]{:S(2)}) collective-permute-start(f32[1,8,8,2,128]{4,3,2,1,0:T(2,128)} %get-tuple-element.19), channel_id=1, source_target_pairs={{16,0},{17,1},{18,2},{19,3},{20,4},{21,5},{22,6},{23,7},{24,8},{25... | collective-permute-start | bytes 196616 | tf_op jit(solution)/shard_map/ppermute | solution.py:12
  10.5 3.4 %copy-start.3 = (f32[192,1,2,128]{3,2,1,0:T(2,128)}, f32[192,1,2,128]{3,2,1,0:T(2,128)S(1)}, u32[]{:S(2)}) copy-start(f32[192,1,2,128]{3,2,1,0:T(2,128)S(1)} %collective-permute-done) | copy-start | bytes 589828
  13.8 0.7 copy-start.5
  16.5 6.4 %copy-start.10 = (f32[6,2]{0,1:T(2,128)S(1)}, f32[6,2]{0,1:T(2,128)}, u32[]{:S(2)}) copy-start(f32[6,2]{0,1:T(2,128)} %param.5) | copy-start | bytes 148
  16.6 7.3 %copy-start = (f32[6,32,8,2,128]{4,3,2,1,0:T(2,128)S(1)}, f32[6,32,8,2,128]{4,3,2,1,0:T(2,128)}, u32[]{:S(2)}) copy-start(f32[6,32,8,2,128]{4,3,2,1,0:T(2,128)} %param.6) | copy-start | bytes 4718596
  18.1 44.1 %collective-permute-start.2 = (f32[192,10,1,128]{3,2,1,0:T(1,128)S(1)}, f32[192,10,1,128]{3,2,1,0:T(1,128)}, u32[]{:S(2)}, u32[]{:S(2)}) collective-permute-start(f32[192,10,1,128]{3,2,1,0:T(1,128)S(1)} %get-tuple-element.4), channel_id=1, source_target_pairs={{1,0},{2,1},{3,2},{4,3},{5,4},{6,5},{7,6},{0,7},{9,8},{10,9},{11,1... | collective-permute-start | bytes 2949128 | tf_op jit(solution)/shard_map/ppermute | solution.py:24
  23.0 39.3 %collective-permute-start.3 = (f32[192,10,1,128]{3,2,1,0:T(1,128)S(1)}, f32[192,10,1,128]{3,2,1,0:T(1,128)}, u32[]{:S(2)}, u32[]{:S(2)}) collective-permute-start(f32[192,10,1,128]{3,2,1,0:T(1,128)S(1)} %get-tuple-element.5), channel_id=1, source_target_pairs={{0,1},{1,2},{2,3},{3,4},{4,5},{5,6},{6,7},{7,0},{8,9},{9,10},{10,1... | collective-permute-start | bytes 2949128 | tf_op jit(solution)/shard_map/ppermute | solution.py:21
  23.1 39.1 %copy-start.8 = (f32[192]{0:T(256)}, f32[192]{0:T(256)S(1)}, u32[]{:S(2)}) copy-start(f32[192]{0:T(256)S(1)} %sub.40) | copy-start | bytes 2308
  26.0 36.3 %copy-start.4 = (f32[192,1,2,128]{3,2,1,0:T(2,128)S(1)}, f32[192,1,2,128]{3,2,1,0:T(2,128)}, u32[]{:S(2)}) copy-start(f32[192,1,2,128]{3,2,1,0:T(2,128)} %copy-done.3) | copy-start | bytes 589828
  26.0 36.3 %copy-start.6 = (f32[192,1,2,128]{3,2,1,0:T(2,128)S(1)}, f32[192,1,2,128]{3,2,1,0:T(2,128)}, u32[]{:S(2)}) copy-start(f32[192,1,2,128]{3,2,1,0:T(2,128)} %copy-done.5) | copy-start | bytes 589828
  62.3 11.3 %copy-start.2 = (f32[6,8,8,2,128]{4,3,2,1,0:T(2,128)S(1)}, f32[6,8,8,2,128]{4,3,2,1,0:T(2,128)}, u32[]{:S(2)}) copy-start(f32[6,8,8,2,128]{4,3,2,1,0:T(2,128)} %param.7) | copy-start | bytes 1179652
  71.5 7.8 %collective-permute-start.4 = (f32[192,1,2,128]{3,2,1,0:T(2,128)S(1)}, f32[192,1,2,128]{3,2,1,0:T(2,128)S(1)}, u32[]{:S(2)}, u32[]{:S(2)}) collective-permute-start(f32[192,1,2,128]{3,2,1,0:T(2,128)S(1)} %get-tuple-element.11), channel_id=1, source_target_pairs={{8,0},{0,8},{9,1},{1,9},{10,2},{2,10},{11,3},{3,11},{12,4},{4,12},... | collective-permute-start | bytes 589832 | tf_op jit(solution)/shard_map/ppermute | solution.py:24
  73.0 9.4 %collective-permute-start.5 = (f32[192,1,2,128]{3,2,1,0:T(2,128)S(1)}, f32[192,1,2,128]{3,2,1,0:T(2,128)S(1)}, u32[]{:S(2)}, u32[]{:S(2)}) collective-permute-start(f32[192,1,2,128]{3,2,1,0:T(2,128)S(1)} %get-tuple-element.10), channel_id=1, source_target_pairs={{0,8},{8,0},{1,9},{9,1},{2,10},{10,2},{3,11},{11,3},{4,12},{12,4},... | collective-permute-start | bytes 589832 | tf_op jit(solution)/shard_map/ppermute | solution.py:21
  86.1 45.1 %collective-permute-start.6 = (f32[192,10,1,128]{3,2,1,0:T(1,128)}, f32[192,10,1,128]{3,2,1,0:T(1,128)}, u32[]{:S(2)}, u32[]{:S(2)}) collective-permute-start(f32[192,10,1,128]{3,2,1,0:T(1,128)} %get-tuple-element.2), channel_id=1, source_target_pairs={{1,0},{2,1},{3,2},{4,3},{5,4},{6,5},{7,6},{0,7},{9,8},{10,9},{11,1... | collective-permute-start | bytes 2949128 | tf_op jit(solution)/shard_map/ppermute | solution.py:24
  88.9 42.3 %collective-permute-start.7 = (f32[192,10,1,128]{3,2,1,0:T(1,128)}, f32[192,10,1,128]{3,2,1,0:T(1,128)}, u32[]{:S(2)}, u32[]{:S(2)}) collective-permute-start(f32[192,10,1,128]{3,2,1,0:T(1,128)} %get-tuple-element.3), channel_id=1, source_target_pairs={{0,1},{1,2},{2,3},{3,4},{4,5},{5,6},{6,7},{7,0},{8,9},{9,10},{10,1... | collective-permute-start | bytes 2949128 | tf_op jit(solution)/shard_map/ppermute | solution.py:21
  95.8 35.3 %copy-start.9 = (f32[192]{0:T(256)S(1)}, f32[192]{0:T(256)}, u32[]{:S(2)}) copy-start(f32[192]{0:T(256)} %copy-done.8) | copy-start | bytes 2308
  141.2 2.6 copy-start.1
  220.3 2.6 copy-start.7
where the time goes:
time: 335 us; the launch traced here: 334 us
  blocking collectives  148 us (44%)
  waiting for transfers between devices  80 us (24%)
  other arithmetic  57.5 us (17%)
  local copies, waits for them, and re-layouts  24.5 us (7%)
  starting transfers between devices  16.2 us (5%)
  matrix products  6.98 us (2%)
    psum x1, blocking collectives, on_device(): lax.psum(jnp.einsum('src,svc->srv', window, filtered, precision=hp), ('lx...  75.1 us
    ppermute x4, waiting for transfers between devices, padded_2(): lax.ppermute(lax.slice_in_dim(block, 0, width, axis=dim), axis, backward)  73.6 us
    psum x1, blocking collectives, on_device(): lax.psum(jnp.einsum('sac,sbc->sab', cleaned, cleaned, precision=hp), ('lx...  72.8 us
    another operation x4, other arithmetic, on_device(): factor = jnp.linalg.cholesky(gram / total)  17.7 us
    another operation x3, other arithmetic, on_device(): result = jax.scipy.linalg.solve_triangular(factor, cleaned, lower=True)  14.9 us
    ppermute x4, starting transfers between devices, padded_2(): lax.ppermute(lax.slice_in_dim(block, 0, width, axis=dim), axis, backward)  12.2 us
    sub x1, other arithmetic, on_device(): previous, current = (current, 2.0 * filter_step(current) - previous)  10.1 us
    div x1, other arithmetic, apply_scaled(): return ((onsite[None] - centre) * inner - beside) / 16.0  9.07 us
  transfers between devices with their start and end apart: 10, of which 6 were waited for; matrix products, arithmetic and copies ran while one was open for 10% of the time, Pallas kernels for 0%

commit v1 on v0

--- a/solution.py
+++ b/solution.py
@@ -58,7 +58,9 @@
     hp = lax.Precision.HIGHEST
     filtered = current.reshape(count, width, cells)
     window = jnp.concatenate([lower, upper], 1).reshape(count, 2 * ritz.shape[1], cells)
-    summed = lax.psum(jnp.einsum("src,svc->srv", window, filtered, precision=hp), ("lx", "ly"))
+    own = jnp.einsum("src,svc->srv", window, filtered, precision=hp)
+    terms = lax.all_gather(own, ("lx", "ly"), axis=0, tiled=False)
+    summed = terms.sum(axis=0)
     correlation = summed / total
     cleaned = filtered - jnp.einsum("srv,src->svc", correlation, window, precision=hp)
     gram = lax.psum(jnp.einsum("sac,sbc->sab", cleaned, cleaned, precision=hp), ("lx", "ly"))

time: 335 us -> 303 us (0.904)
  blocking collectives: 148 us -> 116 us
    psum x1 -> x0, blocking collectives: 75.1 us -> none  [on_device(): lax.psum(jnp.einsum('src,svc->srv', window, filtered, precision=hp), ('lx...]
    all_gather x0 -> x1, blocking collectives: none -> 43.5 us  [on_device(): terms = lax.all_gather(own, ('lx', 'ly'), axis=0, tiled=False)]
  transfers between devices with their start and end apart: 10 -> 10, of which waited for: 6 -> 6; matrix products, arithmetic and copies ran while one was open for 10% -> 11% of each run, Pallas kernels for 0% -> 0%
where the time goes in v1:
time: 303 us; the launch traced here: 302 us
  blocking collectives  116 us (38%)
  waiting for transfers between devices  80 us (26%)
  other arithmetic  57.6 us (19%)
  local copies, waits for them, and re-layouts  24.5 us (8%)
  starting transfers between devices  16.2 us (5%)
  matrix products  6.98 us (2%)
    ppermute x4, waiting for transfers between devices, padded_2(): lax.ppermute(lax.slice_in_dim(block, 0, width, axis=dim), axis, backward)  73.6 us
    psum x1, blocking collectives, on_device(): lax.psum(jnp.einsum('sac,sbc->sab', cleaned, cleaned, precision=hp), ('lx...  72.8 us
    all_gather x1, blocking collectives, on_device(): terms = lax.all_gather(own, ('lx', 'ly'), axis=0, tiled=False)  43.5 us
    another operation x4, other arithmetic, on_device(): factor = jnp.linalg.cholesky(gram / total)  17.7 us
    another operation x3, other arithmetic, on_device(): result = jax.scipy.linalg.solve_triangular(factor, cleaned, lower=True)  14.9 us
    ppermute x4, starting transfers between devices, padded_2(): lax.ppermute(lax.slice_in_dim(block, 0, width, axis=dim), axis, backward)  12.2 us
    sub x1, other arithmetic, on_device(): previous, current = (current, 2.0 * filter_step(current) - previous)  10.1 us
    div x1, other arithmetic, apply_scaled(): return ((onsite[None] - centre) * inner - beside) / 16.0  9.07 us
  transfers between devices with their start and end apart: 10, of which 6 were waited for; matrix products, arithmetic and copies ran while one was open for 11% of the time, Pallas kernels for 0%

profile of v1, /device:TPU:0, one launch (start us, length us, event | category | flops | bytes accessed | tf_op | source)
XLA Modules:
  0.0 302.4 jit_solution(2581995156918181663)
XLA Ops:
  1.7 3.0 %collective-permute-start = (f32[192,1,2,128]{3,2,1,0:T(2,128)S(1)}, f32[192,1,2,128]{3,2,1,0:T(2,128)S(1)}, u32[]{:S(2)}, u32[]{:S(2)}) collective-permute-start(f32[192,1,2,128]{3,2,1,0:T(2,128)S(1)} %get-tuple-element.17), channel_id=1, source_target_pairs={{8,0},{0,8},{9,1},{1,9},{10,2},{2,10},{11,3},{3,11},{12,4},{4,12},... | collective-permute-start | bytes 589832 | tf_op jit(solution)/shard_map/ppermute | solution.py:24
  10.5 3.4 %collective-permute-done.1 = f32[192,1,2,128]{3,2,1,0:T(2,128)S(1)} collective-permute-done((f32[192,1,2,128]{3,2,1,0:T(2,128)S(1)}, f32[192,1,2,128]{3,2,1,0:T(2,128)S(1)}, u32[]{:S(2)}, u32[]{:S(2)}) %collective-permute-start.1) | collective-permute-done | bytes 196640 | tf_op jit(solution)/shard_map/ppermute | solution.py:21
  18.1 4.9 %collective-permute-start.2 = (f32[192,10,1,128]{3,2,1,0:T(1,128)S(1)}, f32[192,10,1,128]{3,2,1,0:T(1,128)}, u32[]{:S(2)}, u32[]{:S(2)}) collective-permute-start(f32[192,10,1,128]{3,2,1,0:T(1,128)S(1)} %get-tuple-element.4), channel_id=1, source_target_pairs={{1,0},{2,1},{3,2},{4,3},{5,4},{6,5},{7,6},{0,7},{9,8},{10,9},{11,1... | collective-permute-start | bytes 2949128 | tf_op jit(solution)/shard_map/ppermute | solution.py:24
  23.8 2.1 fusion.23
  26.0 2.1 fusion.24
  28.2 34.1 %collective-permute-done.2 = f32[192,10,1,128]{3,2,1,0:T(1,128)} collective-permute-done((f32[192,10,1,128]{3,2,1,0:T(1,128)S(1)}, f32[192,10,1,128]{3,2,1,0:T(1,128)}, u32[]{:S(2)}, u32[]{:S(2)}) %collective-permute-start.2) | collective-permute-done | bytes 983072 | tf_op jit(solution)/shard_map/ppermute | solution.py:24
  62.3 9.1 %fusion.1 = f32[192,8,2,128]{3,2,1,0:T(2,128)S(1)} fusion(f32[192,8,2,128]{3,2,1,0:T(2,128)S(1)} %bitcast.25, f32[192,10,1,128]{3,2,1,0:T(1,128)} %collective-permute-done.3, f32[192,1,2,128]{3,2,1,0:T(2,128)S(1)} %copy-done.4, f32[192,1,2,128]{3,2,1,0:T(2,128)S(1)} %copy-done.6, f32[192,10,1,128]{3,2,1,0:T(1,128)} %collective-permute-done.2, ...), kind=kLoop, calls=%fused_computation.6 | loop fusion | flops 7471104 | bytes 8659712 | tf_op jit(solution)/shard_map/div | solution.py:34
  73.8 5.6 %collective-permute-done.4 = f32[192,1,2,128]{3,2,1,0:T(2,128)S(1)} collective-permute-done((f32[192,1,2,128]{3,2,1,0:T(2,128)S(1)}, f32[192,1,2,128]{3,2,1,0:T(2,128)S(1)}, u32[]{:S(2)}, u32[]{:S(2)}) %collective-permute-start.4) | collective-permute-done | bytes 196640 | tf_op jit(solution)/shard_map/ppermute | solution.py:24
  79.3 3.0 %collective-permute-done.5 = f32[192,1,2,128]{3,2,1,0:T(2,128)S(1)} collective-permute-done((f32[192,1,2,128]{3,2,1,0:T(2,128)S(1)}, f32[192,1,2,128]{3,2,1,0:T(2,128)S(1)}, u32[]{:S(2)}, u32[]{:S(2)}) %collective-permute-start.5) | collective-permute-done | bytes 196640 | tf_op jit(solution)/shard_map/ppermute | solution.py:21
  83.3 2.8 fusion.18
  86.1 2.8 collective-permute-start.6
  88.9 2.1 maximum_maximum_fusion
  91.0 2.6 reshape.34
  93.6 2.1 fusion.20
  95.8 2.1 fusion.21
  98.0 33.2 %collective-permute-done.6 = f32[192,10,1,128]{3,2,1,0:T(1,128)} collective-permute-done((f32[192,10,1,128]{3,2,1,0:T(1,128)}, f32[192,10,1,128]{3,2,1,0:T(1,128)}, u32[]{:S(2)}, u32[]{:S(2)}) %collective-permute-start.6) | collective-permute-done | bytes 983072 | tf_op jit(solution)/shard_map/ppermute | solution.py:24
  131.1 10.1 %fusion.4 = f32[192,8,2,128]{3,2,1,0:T(2,128)} fusion(f32[192,8,2,128]{3,2,1,0:T(2,128)S(1)} %fusion.1, f32[192,10,1,128]{3,2,1,0:T(1,128)} %collective-permute-done.7, f32[192,1,2,128]{3,2,1,0:T(2,128)S(1)} %collective-permute-done.4, f32[192,1,2,128]{3,2,1,0:T(2,128)S(1)} %collective-permute-done.5, f32[192,10,1,128]{3,2,1,0:T(1,128)} %collective-permute-done.6, ...), kind=kLoop, calls=%fused_computation.9 | loop fusion | flops 7864320 | bytes 10232576 | tf_op jit(solution)/shard_map/sub | solution.py:54
  141.2 2.6 reshape.33
  145.2 43.5 %all-gather = f32[96,16,32]{2,1,0:T(8,128)S(1)} all-gather(f32[6,16,32]{2,1,0:T(8,128)S(1)} %fusion.28), channel_id=2, replica_groups=mesh['cuts'=2,'lx'=2,'ly'=8] {'lx','ly'}, dimensions={0}, use_global_device_ids=true | all-gather | bytes 208896 | tf_op jit(solution)/shard_map/all_gather | solution.py:62
  188.8 2.6 convolution_subtract_fusion
  192.9 72.8 %psum.7 = f32[6,32,32]{1,2,0:T(8,128)S(1)} all-reduce(f32[6,32,32]{1,2,0:T(8,128)S(1)} %fusion.29), channel_id=1, replica_groups=mesh['cuts'=2,'lx'=2,'ly'=8] {'lx','ly'}, use_global_device_ids=true, to_apply=%region_1.2 | all-reduce | flops 6144 | bytes 49152 | tf_op jit(solution)/shard_map/psum | solution.py:66
  265.8 17.6 %custom-call.8 = f32[6,32,32]{2,1,0:T(8,128)S(1)} custom-call(f32[6,32,32]{2,1,0:T(8,128)S(1)} %fusion.17), custom_call_target="Cholesky" | custom-call | tf_op jit(solution)/shard_map/jit(cholesky)/cholesky | solution.py:67
  283.6 14.8 %custom-call.9 = f32[6,1,32,32]{2,3,1,0:T(8,128)S(1)} custom-call(f32[6,1,32,32]{3,2,1,0:T(8,128)S(1)} %select_bitcast_fusion), custom_call_target="InvertDiagBlocksLowerTriangular" | custom-call | tf_op jit(solution)/shard_map/jit(_solve_triangular)/vmap()/triangular_solve | solution.py:68
  299.9 2.5 reshape.35
  (58 shorter events, 20.0 us)
Async XLA Ops:
  1.7 8.8 %collective-permute-start = (f32[192,1,2,128]{3,2,1,0:T(2,128)S(1)}, f32[192,1,2,128]{3,2,1,0:T(2,128)S(1)}, u32[]{:S(2)}, u32[]{:S(2)}) collective-permute-start(f32[192,1,2,128]{3,2,1,0:T(2,128)S(1)} %get-tuple-element.17), channel_id=1, source_target_pairs={{8,0},{0,8},{9,1},{1,9},{10,2},{2,10},{11,3},{3,11},{12,4},{4,12},... | collective-permute-start | bytes 589832 | tf_op jit(solution)/shard_map/ppermute | solution.py:24
  4.7 9.1 %collective-permute-start.1 = (f32[192,1,2,128]{3,2,1,0:T(2,128)S(1)}, f32[192,1,2,128]{3,2,1,0:T(2,128)S(1)}, u32[]{:S(2)}, u32[]{:S(2)}) collective-permute-start(f32[192,1,2,128]{3,2,1,0:T(2,128)S(1)} %get-tuple-element.16), channel_id=1, source_target_pairs={{0,8},{8,0},{1,9},{9,1},{2,10},{10,2},{3,11},{11,3},{4,12},{12,4},... | collective-permute-start | bytes 589832 | tf_op jit(solution)/shard_map/ppermute | solution.py:21
  6.3 82.5 %collective-permute-start.8 = (f32[1,8,8,2,128]{4,3,2,1,0:T(2,128)}, f32[1,8,8,2,128]{4,3,2,1,0:T(2,128)}, u32[]{:S(2)}, u32[]{:S(2)}) collective-permute-start(f32[1,8,8,2,128]{4,3,2,1,0:T(2,128)} %get-tuple-element.18), channel_id=1, source_target_pairs={{0,16},{1,17},{2,18},{3,19},{4,20},{5,21},{6,22},{7,23},{8,24},{9,... | collective-permute-start | bytes 196616 | tf_op jit(solution)/shard_map/ppermute | solution.py:12
  8.4 80.5 %collective-permute-start.9 = (f32[1,8,8,2,128]{4,3,2,1,0:T(2,128)}, f32[1,8,8,2,128]{4,3,2,1,0:T(2,128)}, u32[]{:S(2)}, u32[]{:S(2)}) collective-permute-start(f32[1,8,8,2,128]{4,3,2,1,0:T(2,128)} %get-tuple-element.19), channel_id=1, source_target_pairs={{16,0},{17,1},{18,2},{19,3},{20,4},{21,5},{22,6},{23,7},{24,8},{25... | collective-permute-start | bytes 196616 | tf_op jit(solution)/shard_map/ppermute | solution.py:12
  10.5 3.4 %copy-start.3 = (f32[192,1,2,128]{3,2,1,0:T(2,128)}, f32[192,1,2,128]{3,2,1,0:T(2,128)S(1)}, u32[]{:S(2)}) copy-start(f32[192,1,2,128]{3,2,1,0:T(2,128)S(1)} %collective-permute-done) | copy-start | bytes 589828
  13.8 0.7 copy-start.5
  16.5 6.4 %copy-start.10 = (f32[6,2]{0,1:T(2,128)S(1)}, f32[6,2]{0,1:T(2,128)}, u32[]{:S(2)}) copy-start(f32[6,2]{0,1:T(2,128)} %param.5) | copy-start | bytes 148
  16.6 7.3 %copy-start = (f32[6,32,8,2,128]{4,3,2,1,0:T(2,128)S(1)}, f32[6,32,8,2,128]{4,3,2,1,0:T(2,128)}, u32[]{:S(2)}) copy-start(f32[6,32,8,2,128]{4,3,2,1,0:T(2,128)} %param.6) | copy-start | bytes 4718596
  18.1 44.1 %collective-permute-start.2 = (f32[192,10,1,128]{3,2,1,0:T(1,128)S(1)}, f32[192,10,1,128]{3,2,1,0:T(1,128)}, u32[]{:S(2)}, u32[]{:S(2)}) collective-permute-start(f32[192,10,1,128]{3,2,1,0:T(1,128)S(1)} %get-tuple-element.4), channel_id=1, source_target_pairs={{1,0},{2,1},{3,2},{4,3},{5,4},{6,5},{7,6},{0,7},{9,8},{10,9},{11,1... | collective-permute-start | bytes 2949128 | tf_op jit(solution)/shard_map/ppermute | solution.py:24
  23.0 39.3 %collective-permute-start.3 = (f32[192,10,1,128]{3,2,1,0:T(1,128)S(1)}, f32[192,10,1,128]{3,2,1,0:T(1,128)}, u32[]{:S(2)}, u32[]{:S(2)}) collective-permute-start(f32[192,10,1,128]{3,2,1,0:T(1,128)S(1)} %get-tuple-element.5), channel_id=1, source_target_pairs={{0,1},{1,2},{2,3},{3,4},{4,5},{5,6},{6,7},{7,0},{8,9},{9,10},{10,1... | collective-permute-start | bytes 2949128 | tf_op jit(solution)/shard_map/ppermute | solution.py:21
  23.1 39.1 %copy-start.8 = (f32[192]{0:T(256)}, f32[192]{0:T(256)S(1)}, u32[]{:S(2)}) copy-start(f32[192]{0:T(256)S(1)} %sub.40) | copy-start | bytes 2308
  26.0 36.3 %copy-start.4 = (f32[192,1,2,128]{3,2,1,0:T(2,128)S(1)}, f32[192,1,2,128]{3,2,1,0:T(2,128)}, u32[]{:S(2)}) copy-start(f32[192,1,2,128]{3,2,1,0:T(2,128)} %copy-done.3) | copy-start | bytes 589828
  26.0 36.3 %copy-start.6 = (f32[192,1,2,128]{3,2,1,0:T(2,128)S(1)}, f32[192,1,2,128]{3,2,1,0:T(2,128)}, u32[]{:S(2)}) copy-start(f32[192,1,2,128]{3,2,1,0:T(2,128)} %copy-done.5) | copy-start | bytes 589828
  62.3 11.3 %copy-start.2 = (f32[6,8,8,2,128]{4,3,2,1,0:T(2,128)S(1)}, f32[6,8,8,2,128]{4,3,2,1,0:T(2,128)}, u32[]{:S(2)}) copy-start(f32[6,8,8,2,128]{4,3,2,1,0:T(2,128)} %param.7) | copy-start | bytes 1179652
  71.5 7.8 %collective-permute-start.4 = (f32[192,1,2,128]{3,2,1,0:T(2,128)S(1)}, f32[192,1,2,128]{3,2,1,0:T(2,128)S(1)}, u32[]{:S(2)}, u32[]{:S(2)}) collective-permute-start(f32[192,1,2,128]{3,2,1,0:T(2,128)S(1)} %get-tuple-element.11), channel_id=1, source_target_pairs={{8,0},{0,8},{9,1},{1,9},{10,2},{2,10},{11,3},{3,11},{12,4},{4,12},... | collective-permute-start | bytes 589832 | tf_op jit(solution)/shard_map/ppermute | solution.py:24
  73.0 9.4 %collective-permute-start.5 = (f32[192,1,2,128]{3,2,1,0:T(2,128)S(1)}, f32[192,1,2,128]{3,2,1,0:T(2,128)S(1)}, u32[]{:S(2)}, u32[]{:S(2)}) collective-permute-start(f32[192,1,2,128]{3,2,1,0:T(2,128)S(1)} %get-tuple-element.10), channel_id=1, source_target_pairs={{0,8},{8,0},{1,9},{9,1},{2,10},{10,2},{3,11},{11,3},{4,12},{12,4},... | collective-permute-start | bytes 589832 | tf_op jit(solution)/shard_map/ppermute | solution.py:21
  86.1 45.1 %collective-permute-start.6 = (f32[192,10,1,128]{3,2,1,0:T(1,128)}, f32[192,10,1,128]{3,2,1,0:T(1,128)}, u32[]{:S(2)}, u32[]{:S(2)}) collective-permute-start(f32[192,10,1,128]{3,2,1,0:T(1,128)} %get-tuple-element.2), channel_id=1, source_target_pairs={{1,0},{2,1},{3,2},{4,3},{5,4},{6,5},{7,6},{0,7},{9,8},{10,9},{11,1... | collective-permute-start | bytes 2949128 | tf_op jit(solution)/shard_map/ppermute | solution.py:24
  88.9 42.3 %collective-permute-start.7 = (f32[192,10,1,128]{3,2,1,0:T(1,128)}, f32[192,10,1,128]{3,2,1,0:T(1,128)}, u32[]{:S(2)}, u32[]{:S(2)}) collective-permute-start(f32[192,10,1,128]{3,2,1,0:T(1,128)} %get-tuple-element.3), channel_id=1, source_target_pairs={{0,1},{1,2},{2,3},{3,4},{4,5},{5,6},{6,7},{7,0},{8,9},{9,10},{10,1... | collective-permute-start | bytes 2949128 | tf_op jit(solution)/shard_map/ppermute | solution.py:21
  95.8 35.3 %copy-start.9 = (f32[192]{0:T(256)S(1)}, f32[192]{0:T(256)}, u32[]{:S(2)}) copy-start(f32[192]{0:T(256)} %copy-done.8) | copy-start | bytes 2308
  141.2 2.6 copy-start.1
  188.8 2.6 copy-start.7
